TPU v7x, 32 devices: a whole 2x2x4 slice. The times are simulated.
32 devices in a mesh: groups: 2 (over x), psg: 16 (over z, y, core).
Axes of the slice: x: 2, y: 2, z: 4, core: 2. Of those that a mesh axis runs over, the one named last changes fastest.
Arguments:
- queries: bfloat16 [64, 32, 128], P(('groups', 'psg')), parts along dimension 0, may hold values from -0.29882812 to 0.29882812
- candidates: int32 [64, 512], P(('groups', 'psg')), parts along dimension 0, may hold values from 0 to 159
- centroids: bfloat16 [8192, 128], P('psg'), may hold values from -6 to 6
- bucket_weights: float32 [4, 128], replicated, may hold values from -1 to 1
- centroid_shard: int32 [32768, 1], P('psg'), may hold values from 0 to 15; in each aligned block of 2048 rows (0 to 2047, 2048 to 4095, ...) at most 256 rows name the same one
- centroid_row: int32 [32768], P('psg'), may hold values from 0 to 511
- residual_codes: int32 [32768, 128], P('psg'), may hold values from 0 to 3
- tile_count: int32 [160], replicated, may hold values from 1 to 3, 256 in all
- last_fill: int32 [160], replicated, may hold values from 1 to 128
Outputs:
- scores: float32 [64, 512], P(('groups', 'psg')), parts along dimension 0
There are 2 independent parts, one for each index of `groups`. A program takes and returns all parts, laid end to end along the dimension named above; an argument that names none is the same for every part. Nothing has to cross between parts.
Inputs may be any that keep to these rules, and one draw needn't show every extreme that they name: `tile_count`: tiles are numbered along psg, device k holding tiles k * 16 onward; the counts sum to 256, so a passage may continue on the next device. `centroid_shard`: among the 2048 token slots of one device, at most 256 name the same device; on some device some value is named exactly 256 times.
All inputs are finite; a program needn't handle non-finite values.
Results may differ from a plain program's by a relative error of at most 0.0003.
Values may be sent and summed in bfloat16 or wider, within the bound.
No kernel may reach another device: no remote copies, remote signals or barrier semaphores. Data moves between devices by JAX's collectives and lax.ppermute only.
A program may use at most 64 MiB of HBM per device.

v0:
```python
import jax
import jax.numpy as jnp
from jax import lax
from jax.sharding import PartitionSpec as P

TILE = 128
epsilon = 1e-06


def tile_layout(tile_count, last_fill, total_tiles, tile_len):
    starts = jnp.cumsum(tile_count) - tile_count
    last_tile = starts + tile_count - 1
    tile_fill = jnp.full((total_tiles,), tile_len, jnp.int32).at[last_tile].set(last_fill)
    return (starts, tile_fill)


def decode(picked, residual_codes, bucket_weights):
    residual = jnp.zeros(residual_codes.shape, jnp.float32)
    for bucket in range(4):
        residual = residual + jnp.where(
            residual_codes == bucket, bucket_weights[bucket][None, :], jnp.float32(0.0)
        )
    summed = picked.astype(jnp.float32) + residual
    scale = lax.rsqrt(jnp.sum(summed * summed, axis=1, keepdims=True) + epsilon)
    return (summed * scale).astype(jnp.bfloat16)


def assemble(own_maxima, candidates, starts, total_tiles, query_len):
    num_queries, num_cand = candidates.shape
    marker = jnp.zeros((total_tiles,), jnp.int32).at[starts].add(1)
    owner_id = jnp.cumsum(marker)
    same_next = jnp.concatenate([owner_id[1:] == owner_id[:-1], jnp.zeros((1,), bool)])
    same_after = jnp.concatenate([owner_id[2:] == owner_id[:-2], jnp.zeros((2,), bool)])
    shifted_one = jnp.concatenate([own_maxima[:, 1:], own_maxima[:, :1]], axis=1)
    shifted_two = jnp.concatenate([own_maxima[:, 2:], own_maxima[:, :2]], axis=1)
    combined = jnp.maximum(own_maxima, jnp.where(same_next[None, :], shifted_one, own_maxima))
    combined = jnp.maximum(combined, jnp.where(same_after[None, :], shifted_two, own_maxima))
    combined = combined.reshape(num_queries, query_len, total_tiles)
    first_tile = starts[candidates]
    selector = (
        first_tile[:, :, None] == jnp.arange(total_tiles, dtype=jnp.int32)[None, None, :]
    ).astype(jnp.float32)
    return jnp.einsum(
        "qit,qct->qc",
        combined,
        selector,
        precision=lax.Precision.HIGHEST,
        preferred_element_type=jnp.float32,
    )


def per_device(
    queries,
    candidates,
    centroids,
    bucket_weights,
    centroid_shard,
    centroid_row,
    residual_codes,
    tile_count,
    last_fill,
):
    n_psg = lax.axis_size("psg")
    shard_index = lax.axis_index("psg")
    tok_dev = residual_codes.shape[0]
    tiles_dev = tok_dev // TILE
    cent_dev = centroids.shape[0]
    owners = centroid_shard[:, 0]
    codebook = lax.all_gather(centroids, "psg", axis=0, tiled=True)
    picked = jnp.take(codebook, owners * cent_dev + centroid_row, axis=0)
    embedded = decode(picked, residual_codes, bucket_weights)
    total_tiles = tiles_dev * n_psg
    starts, tile_fill = tile_layout(tile_count, last_fill, total_tiles, TILE)
    local_fill = lax.dynamic_slice_in_dim(tile_fill, shard_index * tiles_dev, tiles_dev, 0)
    token_mask = jnp.arange(TILE, dtype=jnp.int32)[None, :] < local_fill[:, None]
    pad_bias = jnp.where(token_mask, jnp.float32(0.0), -jnp.inf).reshape(-1)
    per_block = max(1, 512 // TILE)
    while tiles_dev % per_block:
        per_block -= 1
    width = per_block * TILE
    piece = lax.all_gather(queries, "psg", axis=0, tiled=True)
    flat_rows = piece.reshape(-1, piece.shape[-1])
    pieces = []
    for block in range(tiles_dev // per_block):
        key_block = embedded[block * width : (block + 1) * width]
        block_scores = jnp.einsum(
            "qd,kd->qk", flat_rows, key_block, preferred_element_type=jnp.float32
        )
        block_scores = block_scores + pad_bias[block * width : (block + 1) * width][None, :]
        pieces.append(jnp.max(block_scores.reshape(flat_rows.shape[0], per_block, TILE), axis=2))
    maxima = jnp.concatenate(pieces, axis=1)
    own_maxima = lax.all_to_all(maxima, "psg", split_axis=0, concat_axis=1, tiled=True)
    return assemble(own_maxima, candidates, starts, total_tiles, queries.shape[1])


def solution(mesh):
    placed = (
        P(("groups", "psg"), None, None),
        P(("groups", "psg"), None),
        P("psg", None),
        P(),
        P("psg", None),
        P("psg"),
        P("psg", None),
        P(),
        P(),
    )
    return jax.shard_map(
        per_device,
        mesh=mesh,
        in_specs=placed,
        out_specs=P(("groups", "psg"), None),
        check_vma=False,
    )
```

profile of v0, /device:TPU:0, one launch (start us, length us, event | category | flops | bytes accessed | tf_op | source)
XLA Modules:
  0.0 90.6 jit_solution(17494278856567617430)
XLA Ops:
  6.5 0.0 all-gather.2.cloned.1.call-start
  6.5 0.7 all-gather.2.cloned.1.call-update
  7.3 0.7 pad_bitcast_fusion
  7.9 0.3 reduce-window.16
  8.3 0.1 slice.84
  8.4 0.1 slice_reduce_fusion.1
  8.5 0.1 add_bitcast_fusion.1
  8.6 0.7 compare_select_fusion.2
  9.2 1.7 %scatter_custom_fusion.1 = s32[256]{0:T(256)S(1)} fusion(s32[160]{0:T(256)S(1)} %get-tuple-element.5, s32[160]{0:T(256)S(1)} %broadcast.58, s32[]{:T(128)} %constant.21.clone.1), kind=kCustom, calls=%fused_computation.54 | custom fusion | flops 160 | bytes 1028 | tf_op jit(solution)/shard_map/scatter-add | solution.py:30
  10.9 0.3 reduce-window.24
  11.2 0.1 slice.93
  11.3 0.7 fusion.9
  12.0 1.2 %scatter_custom_fusion = s32[256]{0:T(256)S(1)} fusion(s32[160]{0:T(256)S(1)} %get-tuple-element.17, s32[160]{0:T(256)} %param.17, s32[]{:T(128)} %constant.15.clone.1), kind=kCustom, calls=%fused_computation.56 | custom fusion | bytes 1536 | tf_op jit(solution)/shard_map/scatter | solution.py:13
  13.3 0.1 dynamic_slice.3
  13.4 0.1 slice_reduce_fusion
  13.5 24.3 %all_gather.7 = bf16[32,32,128]{2,1,0:T(8,128)(2,1)S(1)} all-gather(bf16[2,32,128]{2,1,0:T(8,128)(2,1)} %param.9), channel_id=1, replica_groups=mesh['groups'=2,'psg'=16] {'psg'}, dimensions={0}, use_global_device_ids=true | all-gather | bytes 278528 | tf_op jit(solution)/shard_map/all_gather | solution.py:81
  37.8 0.1 add_bitcast_fusion
  37.9 0.1 slice_compare_fusion
  38.0 0.8 slice_bitcast_fusion.7
  38.8 0.1 fusion.8
  38.9 0.7 broadcast_multiply_fusion
  39.6 0.7 compare_and_fusion
  40.3 0.7 broadcast_clamp_fusion
  41.0 0.0 copy-start
  41.0 13.0 %all-gather.2.cloned.1.call-done = bf16[8192,128]{1,0:T(8,128)(2,1)} async-done(((bf16[512,128]{1,0:T(8,128)(2,1)}), bf16[8192,128]{1,0:T(8,128)(2,1)}) %all-gather.2.cloned.1.call-update) | async-done | bytes 2097168 | tf_op jit(solution)/shard_map/all_gather | solution.py:69
  54.0 7.5 %gather_fusion = bf16[2048,128]{1,0:T(8,128)(2,1)S(1)} fusion(bf16[8192,128]{1,0:T(8,128)(2,1)} %all-gather.2.cloned.1.call-done, s32[2048]{0:T(1024)S(1)} %broadcast_clamp_fusion), kind=kCustom, calls=%fused_computation | custom fusion | bytes 1056768 | tf_op jit(solution)/shard_map/jit(_take)/gather | solution.py:70
  61.5 0.0 copy-done
  61.5 0.9 multiply_reduce_fusion
  62.4 0.3 multiply_convert_fusion
  62.8 0.5 bitcast_reduce_fusion.3
  63.2 0.5 bitcast_reduce_fusion.2
  63.7 0.5 bitcast_reduce_fusion.1
  64.2 0.5 bitcast_reduce_fusion
  64.6 0.1 all_to_all.16
  64.8 0.7 reshape.153
  65.5 3.5 %all-to-all-start = ((f32[16,1,1024]{2,1,0:T(1,128)}), f32[16,1,1024]{2,1,0:T(1,128)S(1)}, u32[]{:S(2)}, u32[]{:S(2)}) async-start(f32[16,1,1024]{2,1,0:T(1,128)} %reshape.153), calls=%async_computation | async-start | bytes 131072 | tf_op jit(solution)/shard_map/all_to_all | solution.py:92
  69.0 0.1 slice_compare_fusion.1
  69.1 6.8 %gather_fusion.1 = s32[1024]{0:T(1024)S(1)} fusion(s32[160]{0:T(256)S(1)} %get-tuple-element.6, s32[1024]{0:T(1024)S(1)} %broadcast_clamp_fusion.1), kind=kCustom, calls=%fused_computation.1 | custom fusion | bytes 12288 | tf_op jit(solution)/shard_map/gather | solution.py:39
  76.0 0.1 pad_add_fusion
  76.0 0.0 all-to-all-done
  76.0 0.5 broadcast.78
  76.6 0.8 reduce.8
  77.4 0.1 reshape.154
  77.5 0.1 copy.28
  77.6 0.2 copy.29
  77.8 0.1 copy.30
  77.9 0.2 copy.31
  78.0 0.2 all_to_all.19
  78.2 0.1 concatenate.32
  78.3 0.1 concatenate.28
  78.4 4.0 %fusion.3 = f32[2,256]{0,1:T(8,128)S(1)} fusion(f32[2,32,256]{1,0,2:T(2,128)S(1)} %all_to_all.19, f32[2,32,1]{1,0,2:T(2,128)S(1)} %concatenate.28, f32[2,32,255]{1,0,2:T(2,128)S(1)} %copy.29, f32[2,32,2]{1,0,2:T(2,128)S(1)} %concatenate.32, f32[2,32,254]{1,0,2:T(2,128)S(1)} %copy.31, pred[256]{0:T(512)(128)(4,1)S(1)} %concatenate.30, ...), kind=kLoop, calls=%fused_computation.20 | loop fusion | flops 114176 | bytes 199168 | tf_op jit(solution)/shard_map/qit,qct->qc/reduce_sum | solution.py:43
  82.4 0.1 copy.32
  82.5 0.6 fusion
  83.1 0.6 copy.37
  (16 shorter events, 0.2 us)
Async XLA Ops:
  6.5 47.5 %all-gather.2.cloned.1.call-start = ((), (), s32[]{:S(2)}) async-start(), calls=%async_computation.1 | async-start | bytes 2228224 | tf_op jit(solution)/shard_map/all_gather | solution.py:69
  41.0 20.5 %copy-start = (s32[2048,128]{1,0:T(8,128)S(1)}, s32[2048,128]{1,0:T(8,128)}, u32[]{:S(2)}) copy-start(s32[2048,128]{1,0:T(8,128)} %param.15) | copy-start | bytes 3145732
  65.5 10.5 %all-to-all-start = ((f32[16,1,1024]{2,1,0:T(1,128)}), f32[16,1,1024]{2,1,0:T(1,128)S(1)}, u32[]{:S(2)}, u32[]{:S(2)}) async-start(f32[16,1,1024]{2,1,0:T(1,128)} %reshape.153), calls=%async_computation | async-start | bytes 131072 | tf_op jit(solution)/shard_map/all_to_all | solution.py:92
Sparse Core Ops, SparseCore 0:
  9.5 44.4 all-gather.1
where the time goes:
time: 91.1 us; the launch traced here: 90.6 us
  blocking collectives  24.3 us (27%)
  local copies, waits for them, and re-layouts  20.6 us (23%)
  waiting for transfers between devices  13.8 us (15%)
  between operations  13.6 us (15%)
  other arithmetic  12.4 us (14%)
  starting transfers between devices  3.5 us (4%)
  matrix products  2.45 us (3%)
    all_gather x1, blocking collectives, per_device(): piece = lax.all_gather(queries, 'psg', axis=0, tiled=True)  24.3 us
    all_gather x1, waiting for transfers between devices, per_device(): codebook = lax.all_gather(centroids, 'psg', axis=0, tiled=True)  13 us
    gather x1, local copies, waits for them, and re-layouts, per_device(): picked = jnp.take(codebook, owners * cent_dev + centroid_row, axis=0)  7.45 us
    gather x2, local copies, waits for them, and re-layouts, assemble(): first_tile = starts[candidates]  6.83 us
    reduce_sum x1, other arithmetic, assemble(): jnp.einsum('qit,qct->qc', combined, selector, precision=lax.Precision.HIG...  4.02 us
    all_to_all x1, starting transfers between devices, per_device(): lax.all_to_all(maxima, 'psg', split_axis=0, concat_axis=1, tiled=True)  3.5 us
    dot_general x4, matrix products, per_device(): jnp.einsum('qd,kd->qk', flat_rows, key_block, preferred_element_type=jnp....  1.83 us
  transfers between devices with their start and end apart: 2, of which 1 were waited for; matrix products, arithmetic and copies ran while one was open for 18% of the time, Pallas kernels for 0%

commit v1 on v0

--- a/solution.py
+++ b/solution.py
@@ -78,7 +78,16 @@
     while tiles_dev % per_block:
         per_block -= 1
     width = per_block * TILE
-    piece = lax.all_gather(queries, "psg", axis=0, tiled=True)
+    ways = lax.axis_size("psg")
+    up = [(d, (d + 1) % ways) for d in range(ways)]
+    down = [(d, (d - 1) % ways) for d in range(ways)]
+    earlier, later = ([queries], [queries])
+    for _ in range(ways // 2):
+        earlier.append(lax.ppermute(earlier[-1], "psg", up))
+    for _ in range((ways - 1) // 2):
+        later.append(lax.ppermute(later[-1], "psg", down))
+    line = jnp.concatenate([*earlier[::-1], *later[1:]], axis=0)
+    piece = jnp.roll(line, (lax.axis_index("psg") - ways // 2) * queries.shape[0], axis=0)
     flat_rows = piece.reshape(-1, piece.shape[-1])
     pieces = []
     for block in range(tiles_dev // per_block):

time: 91.1 us -> 102 us (1.12)
  starting transfers between devices: 3.5 us -> 38 us
  blocking collectives: 24.3 us -> 0 us
  local copies, waits for them, and re-layouts: 20.6 us -> 22.4 us
    ppermute x0 -> x15, starting transfers between devices: none -> 32.2 us  [the longest x7 31.7 us: per_device(): later.append(lax.ppermute(later[-1], 'psg', down))]
    all_gather x1 -> x0, blocking collectives: 24.3 us -> none  [per_device(): piece = lax.all_gather(queries, 'psg', axis=0, tiled=True)]
    all_gather x1, waiting for transfers between devices: 13 us -> 0.02 us  [per_device(): codebook = lax.all_gather(centroids, 'psg', axis=0, tiled=True)]
    ppermute x0 -> x15, waiting for transfers between devices: none -> 12.7 us  [the longest x8 8.32 us: per_device(): earlier.append(lax.ppermute(earlier[-1], 'psg', up))]
    all_to_all x1, starting transfers between devices: 3.5 us -> 5.8 us  [per_device(): lax.all_to_all(maxima, 'psg', split_axis=0, concat_axis=1, tiled=True)]
    unnamed x5 -> x36, local copies, waits for them, and re-layouts: 0.84 us -> 2.54 us
  transfers between devices with their start and end apart: 2 -> 17, of which waited for: 1 -> 11; matrix products, arithmetic and copies ran while one was open for 18% -> 18% of each run, Pallas kernels for 0% -> 0%
where the time goes in v1:
time: 102 us
  starting transfers between devices  38 us (37%)
  local copies, waits for them, and re-layouts  22.4 us (22%)
  between operations  13.7 us (13%)
  waiting for transfers between devices  12.8 us (13%)
  other arithmetic  12.4 us (12%)
  matrix products  2.44 us (2%)
    ppermute x7, starting transfers between devices, per_device(): later.append(lax.ppermute(later[-1], 'psg', down))  31.7 us
    ppermute x8, waiting for transfers between devices, per_device(): earlier.append(lax.ppermute(earlier[-1], 'psg', up))  8.32 us
    gather x1, local copies, waits for them, and re-layouts, per_device(): picked = jnp.take(codebook, owners * cent_dev + centroid_row, axis=0)  7.55 us
    gather x2, local copies, waits for them, and re-layouts, assemble(): first_tile = starts[candidates]  6.86 us
    all_to_all x1, starting transfers between devices, per_device(): lax.all_to_all(maxima, 'psg', split_axis=0, concat_axis=1, tiled=True)  5.8 us
    ppermute x7, waiting for transfers between devices, per_device(): later.append(lax.ppermute(later[-1], 'psg', down))  4.42 us
    reduce_sum x1, other arithmetic, assemble(): jnp.einsum('qit,qct->qc', combined, selector, precision=lax.Precision.HIG...  4.03 us
    unnamed x36, local copies, waits for them, and re-layouts  2.54 us
  transfers between devices with their start and end apart: 17, of which 11 were waited for; matrix products, arithmetic and copies ran while one was open for 18% of the time, Pallas kernels for 0%

profile of v1, /device:TPU:0, one launch (start us, length us, event | category | flops | bytes accessed | tf_op | source)
XLA Modules:
  0.0 101.8 jit_solution(17796609016214343100)
XLA Ops:
  6.5 0.5 collective-permute-start
  7.0 5.0 %collective-permute-start.8 = (bf16[2,32,128]{2,1,0:T(8,128)(2,1)}, bf16[2,32,128]{2,1,0:T(8,128)(2,1)S(1)}, u32[]{:S(2)}, u32[]{:S(2)}) collective-permute-start(bf16[2,32,128]{2,1,0:T(8,128)(2,1)} %param.9), channel_id=1, source_target_pairs={{0,15},{1,0},{2,1},{3,2},{4,3},{5,4},{6,5},{7,6},{8,7},{9,8},{10,9... | collective-permute-start | bytes 49160 | tf_op jit(solution)/shard_map/ppermute | solution.py:88
  12.0 0.7 broadcast_multiply_fusion
  12.7 0.7 compare_and_fusion
  13.5 0.7 broadcast_clamp_fusion
  14.2 0.7 pad_bitcast_fusion
  14.8 0.3 reduce-window.16
  15.1 0.1 slice.84
  15.3 0.1 slice_reduce_fusion.1
  15.5 0.7 compare_select_fusion.2
  16.1 1.2 %scatter_custom_fusion = s32[256]{0:T(256)S(1)} fusion(s32[160]{0:T(256)S(1)} %get-tuple-element.17, s32[160]{0:T(256)} %param.17, s32[]{:T(128)} %constant.79.clone.1), kind=kCustom, calls=%fused_computation.88 | custom fusion | bytes 1536 | tf_op jit(solution)/shard_map/scatter | solution.py:13
  17.4 0.1 dynamic_slice.8
  17.6 5.9 %collective-permute-done.1 = bf16[2,32,128]{2,1,0:T(8,128)(2,1)S(1)} collective-permute-done((bf16[2,32,128]{2,1,0:T(8,128)(2,1)S(1)}, bf16[2,32,128]{2,1,0:T(8,128)(2,1)S(1)}, u32[]{:S(2)}, u32[]{:S(2)}) %collective-permute-start.1) | collective-permute-done | bytes 16416 | tf_op jit(solution)/shard_map/ppermute | solution.py:86
  23.5 0.7 fusion.9
  24.2 4.5 %collective-permute-start.9 = (bf16[2,32,128]{2,1,0:T(8,128)(2,1)S(1)}, bf16[2,32,128]{2,1,0:T(8,128)(2,1)S(1)}, u32[]{:S(2)}, u32[]{:S(2)}) collective-permute-start(bf16[2,32,128]{2,1,0:T(8,128)(2,1)S(1)} %collective-permute-done.8), channel_id=1, source_target_pairs={{0,15},{1,0},{2,1},{3,2},{4,3},{5,4},{6,5},{7,6},{8,7},{9,8},{10,9... | collective-permute-start | bytes 49160 | tf_op jit(solution)/shard_map/ppermute | solution.py:88
  28.7 0.8 collective-permute-done.2
  29.6 0.6 collective-permute-done.9
  30.2 4.5 %collective-permute-start.10 = (bf16[2,32,128]{2,1,0:T(8,128)(2,1)S(1)}, bf16[2,32,128]{2,1,0:T(8,128)(2,1)S(1)}, u32[]{:S(2)}, u32[]{:S(2)}) collective-permute-start(bf16[2,32,128]{2,1,0:T(8,128)(2,1)S(1)} %collective-permute-done.9), channel_id=1, source_target_pairs={{0,15},{1,0},{2,1},{3,2},{4,3},{5,4},{6,5},{7,6},{8,7},{9,8},{10,9... | collective-permute-start | bytes 49160 | tf_op jit(solution)/shard_map/ppermute | solution.py:88
  34.7 0.7 collective-permute-done.3
  35.4 0.8 slice_bitcast_fusion.7
  36.2 1.7 %scatter_custom_fusion.1 = s32[256]{0:T(256)S(1)} fusion(s32[160]{0:T(256)S(1)} %get-tuple-element.5, s32[160]{0:T(256)S(1)} %broadcast.55, s32[]{:T(128)} %constant.38.clone.1), kind=kCustom, calls=%fused_computation.86 | custom fusion | flops 160 | bytes 1028 | tf_op jit(solution)/shard_map/scatter-add | solution.py:30
  37.9 0.3 reduce-window.24
  38.2 0.1 slice.93
  38.3 4.5 %collective-permute-start.11 = (bf16[2,32,128]{2,1,0:T(8,128)(2,1)S(1)}, bf16[2,32,128]{2,1,0:T(8,128)(2,1)S(1)}, u32[]{:S(2)}, u32[]{:S(2)}) collective-permute-start(bf16[2,32,128]{2,1,0:T(8,128)(2,1)S(1)} %collective-permute-done.10), channel_id=1, source_target_pairs={{0,15},{1,0},{2,1},{3,2},{4,3},{5,4},{6,5},{7,6},{8,7},{9,8},{10,9... | collective-permute-start | bytes 49160 | tf_op jit(solution)/shard_map/ppermute | solution.py:88
  42.8 0.1 slice_reduce_fusion
  42.9 1.3 %collective-permute-done.11 = bf16[2,32,128]{2,1,0:T(8,128)(2,1)S(1)} collective-permute-done((bf16[2,32,128]{2,1,0:T(8,128)(2,1)S(1)}, bf16[2,32,128]{2,1,0:T(8,128)(2,1)S(1)}, u32[]{:S(2)}, u32[]{:S(2)}) %collective-permute-start.11) | collective-permute-done | bytes 16416 | tf_op jit(solution)/shard_map/ppermute | solution.py:88
  44.3 4.4 %collective-permute-start.12 = (bf16[2,32,128]{2,1,0:T(8,128)(2,1)S(1)}, bf16[2,32,128]{2,1,0:T(8,128)(2,1)S(1)}, u32[]{:S(2)}, u32[]{:S(2)}) collective-permute-start(bf16[2,32,128]{2,1,0:T(8,128)(2,1)S(1)} %collective-permute-done.11), channel_id=1, source_target_pairs={{0,15},{1,0},{2,1},{3,2},{4,3},{5,4},{6,5},{7,6},{8,7},{9,8},{10,9... | collective-permute-start | bytes 49160 | tf_op jit(solution)/shard_map/ppermute | solution.py:88
  48.7 0.3 collective-permute-done.5
  49.0 1.1 %collective-permute-done.12 = bf16[2,32,128]{2,1,0:T(8,128)(2,1)S(1)} collective-permute-done((bf16[2,32,128]{2,1,0:T(8,128)(2,1)S(1)}, bf16[2,32,128]{2,1,0:T(8,128)(2,1)S(1)}, u32[]{:S(2)}, u32[]{:S(2)}) %collective-permute-start.12) | collective-permute-done | bytes 16416 | tf_op jit(solution)/shard_map/ppermute | solution.py:88
  50.1 4.4 %collective-permute-start.13 = (bf16[2,32,128]{2,1,0:T(8,128)(2,1)S(1)}, bf16[2,32,128]{2,1,0:T(8,128)(2,1)S(1)}, u32[]{:S(2)}, u32[]{:S(2)}) collective-permute-start(bf16[2,32,128]{2,1,0:T(8,128)(2,1)S(1)} %collective-permute-done.12), channel_id=1, source_target_pairs={{0,15},{1,0},{2,1},{3,2},{4,3},{5,4},{6,5},{7,6},{8,7},{9,8},{10,9... | collective-permute-start | bytes 49160 | tf_op jit(solution)/shard_map/ppermute | solution.py:88
  54.5 0.3 collective-permute-done.6
  54.8 0.1 slice_compare_fusion.1
  54.9 1.1 %collective-permute-done.13 = bf16[2,32,128]{2,1,0:T(8,128)(2,1)S(1)} collective-permute-done((bf16[2,32,128]{2,1,0:T(8,128)(2,1)S(1)}, bf16[2,32,128]{2,1,0:T(8,128)(2,1)S(1)}, u32[]{:S(2)}, u32[]{:S(2)}) %collective-permute-start.13) | collective-permute-done | bytes 16416 | tf_op jit(solution)/shard_map/ppermute | solution.py:88
  56.0 4.4 %collective-permute-start.14 = (bf16[2,32,128]{2,1,0:T(8,128)(2,1)S(1)}, bf16[2,32,128]{2,1,0:T(8,128)(2,1)S(1)}, u32[]{:S(2)}, u32[]{:S(2)}) collective-permute-start(bf16[2,32,128]{2,1,0:T(8,128)(2,1)S(1)} %collective-permute-done.13), channel_id=1, source_target_pairs={{0,15},{1,0},{2,1},{3,2},{4,3},{5,4},{6,5},{7,6},{8,7},{9,8},{10,9... | collective-permute-start | bytes 49160 | tf_op jit(solution)/shard_map/ppermute | solution.py:88
  60.4 0.3 collective-permute-done.7
  60.8 0.7 constant_dynamic-update-slice_fusion.23
  61.5 0.3 collective-permute-done.14
  61.9 0.7 constant_dynamic-update-slice_fusion.7
  62.8 7.6 %gather_fusion = bf16[2048,128]{1,0:T(8,128)(2,1)S(1)} fusion(bf16[8192,128]{1,0:T(8,128)(2,1)} %all-gather.2.cloned.1.call-done, s32[2048]{0:T(1024)S(1)} %broadcast_clamp_fusion), kind=kCustom, calls=%fused_computation | custom fusion | bytes 1056768 | tf_op jit(solution)/shard_map/jit(_take)/gather | solution.py:70
  70.4 0.9 multiply_reduce_fusion
  71.3 0.3 multiply_convert_fusion
  71.6 0.5 bitcast_reduce_fusion
  72.1 0.5 bitcast_reduce_fusion.1
  72.6 0.5 bitcast_reduce_fusion.2
  73.0 0.5 bitcast_reduce_fusion.3
  73.5 0.1 all_to_all.16
  73.6 0.7 reshape.153
  74.4 5.8 %all-to-all-start = ((f32[16,1,1024]{2,1,0:T(1,128)}), f32[16,1,1024]{2,1,0:T(1,128)S(1)}, u32[]{:S(2)}, u32[]{:S(2)}) async-start(f32[16,1,1024]{2,1,0:T(1,128)} %reshape.153), calls=%async_computation | async-start | bytes 131072 | tf_op jit(solution)/shard_map/all_to_all | solution.py:101
  80.2 0.1 slice_compare_fusion
  80.3 6.9 %gather_fusion.1 = s32[1024]{0:T(1024)S(1)} fusion(s32[160]{0:T(256)S(1)} %get-tuple-element.6, s32[1024]{0:T(1024)S(1)} %broadcast_clamp_fusion.1), kind=kCustom, calls=%fused_computation.1 | custom fusion | bytes 12288 | tf_op jit(solution)/shard_map/gather | solution.py:39
  87.2 0.1 pad_add_fusion
  87.2 0.5 broadcast.75
  87.8 0.8 reduce.8
  88.6 0.1 reshape.154
  88.7 0.1 concatenate.35
  88.8 0.1 concatenate.39
  88.9 0.1 copy.30
  89.0 0.1 copy.28
  89.1 0.2 all_to_all.19
  89.3 0.2 copy.31
  89.4 0.2 copy.29
  89.6 4.0 %fusion.3 = f32[2,256]{0,1:T(8,128)S(1)} fusion(f32[2,32,256]{1,0,2:T(2,128)S(1)} %all_to_all.19, f32[2,32,1]{1,0,2:T(2,128)S(1)} %concatenate.35, f32[2,32,255]{1,0,2:T(2,128)S(1)} %copy.29, f32[2,32,2]{1,0,2:T(2,128)S(1)} %concatenate.39, f32[2,32,254]{1,0,2:T(2,128)S(1)} %copy.31, pred[256]{0:T(512)(128)(4,1)S(1)} %concatenate.37, ...), kind=kLoop, calls=%fused_computation.20 | loop fusion | flops 114176 | bytes 199168 | tf_op jit(solution)/shard_map/qit,qct->qc/reduce_sum | solution.py:43
  93.7 0.6 fusion
  94.3 0.6 copy.37
  (68 shorter events, 0.9 us)
Async XLA Ops:
  6.5 56.3 %all-gather.2.cloned.1.call-start = ((), (), s32[]{:S(2)}) async-start(), calls=%async_computation.1 | async-start | bytes 2228224 | tf_op jit(solution)/shard_map/all_gather | solution.py:69
  6.5 11.0 %collective-permute-start = (bf16[2,32,128]{2,1,0:T(8,128)(2,1)}, bf16[2,32,128]{2,1,0:T(8,128)(2,1)S(1)}, u32[]{:S(2)}, u32[]{:S(2)}) collective-permute-start(bf16[2,32,128]{2,1,0:T(8,128)(2,1)} %param.9), channel_id=1, source_target_pairs={{0,1},{1,2},{2,3},{3,4},{4,5},{5,6},{6,7},{7,8},{8,9},{9,10},{10,1... | collective-permute-start | bytes 49160 | tf_op jit(solution)/shard_map/ppermute | solution.py:86
  7.0 17.2 %collective-permute-start.8 = (bf16[2,32,128]{2,1,0:T(8,128)(2,1)}, bf16[2,32,128]{2,1,0:T(8,128)(2,1)S(1)}, u32[]{:S(2)}, u32[]{:S(2)}) collective-permute-start(bf16[2,32,128]{2,1,0:T(8,128)(2,1)} %param.9), channel_id=1, source_target_pairs={{0,15},{1,0},{2,1},{3,2},{4,3},{5,4},{6,5},{7,6},{8,7},{9,8},{10,9... | collective-permute-start | bytes 49160 | tf_op jit(solution)/shard_map/ppermute | solution.py:88
  17.5 6.0 %collective-permute-start.1 = (bf16[2,32,128]{2,1,0:T(8,128)(2,1)S(1)}, bf16[2,32,128]{2,1,0:T(8,128)(2,1)S(1)}, u32[]{:S(2)}, u32[]{:S(2)}) collective-permute-start(bf16[2,32,128]{2,1,0:T(8,128)(2,1)S(1)} %collective-permute-done), channel_id=1, source_target_pairs={{0,1},{1,2},{2,3},{3,4},{4,5},{5,6},{6,7},{7,8},{8,9},{9,10},{10,1... | collective-permute-start | bytes 49160 | tf_op jit(solution)/shard_map/ppermute | solution.py:86
  23.5 6.0 %collective-permute-start.2 = (bf16[2,32,128]{2,1,0:T(8,128)(2,1)S(1)}, bf16[2,32,128]{2,1,0:T(8,128)(2,1)S(1)}, u32[]{:S(2)}, u32[]{:S(2)}) collective-permute-start(bf16[2,32,128]{2,1,0:T(8,128)(2,1)S(1)} %collective-permute-done.1), channel_id=1, source_target_pairs={{0,1},{1,2},{2,3},{3,4},{4,5},{5,6},{6,7},{7,8},{8,9},{9,10},{10,1... | collective-permute-start | bytes 49160 | tf_op jit(solution)/shard_map/ppermute | solution.py:86
  24.2 5.9 %collective-permute-start.9 = (bf16[2,32,128]{2,1,0:T(8,128)(2,1)S(1)}, bf16[2,32,128]{2,1,0:T(8,128)(2,1)S(1)}, u32[]{:S(2)}, u32[]{:S(2)}) collective-permute-start(bf16[2,32,128]{2,1,0:T(8,128)(2,1)S(1)} %collective-permute-done.8), channel_id=1, source_target_pairs={{0,15},{1,0},{2,1},{3,2},{4,3},{5,4},{6,5},{7,6},{8,7},{9,8},{10,9... | collective-permute-start | bytes 49160 | tf_op jit(solution)/shard_map/ppermute | solution.py:88
  29.5 5.9 %collective-permute-start.3 = (bf16[2,32,128]{2,1,0:T(8,128)(2,1)S(1)}, bf16[2,32,128]{2,1,0:T(8,128)(2,1)S(1)}, u32[]{:S(2)}, u32[]{:S(2)}) collective-permute-start(bf16[2,32,128]{2,1,0:T(8,128)(2,1)S(1)} %collective-permute-done.2), channel_id=1, source_target_pairs={{0,1},{1,2},{2,3},{3,4},{4,5},{5,6},{6,7},{7,8},{8,9},{9,10},{10,1... | collective-permute-start | bytes 49160 | tf_op jit(solution)/shard_map/ppermute | solution.py:86
  30.2 8.2 %collective-permute-start.10 = (bf16[2,32,128]{2,1,0:T(8,128)(2,1)S(1)}, bf16[2,32,128]{2,1,0:T(8,128)(2,1)S(1)}, u32[]{:S(2)}, u32[]{:S(2)}) collective-permute-start(bf16[2,32,128]{2,1,0:T(8,128)(2,1)S(1)} %collective-permute-done.9), channel_id=1, source_target_pairs={{0,15},{1,0},{2,1},{3,2},{4,3},{5,4},{6,5},{7,6},{8,7},{9,8},{10,9... | collective-permute-start | bytes 49160 | tf_op jit(solution)/shard_map/ppermute | solution.py:88
  35.4 7.4 %collective-permute-start.4 = (bf16[2,32,128]{2,1,0:T(8,128)(2,1)S(1)}, bf16[2,32,128]{2,1,0:T(8,128)(2,1)S(1)}, u32[]{:S(2)}, u32[]{:S(2)}) collective-permute-start(bf16[2,32,128]{2,1,0:T(8,128)(2,1)S(1)} %collective-permute-done.3), channel_id=1, source_target_pairs={{0,1},{1,2},{2,3},{3,4},{4,5},{5,6},{6,7},{7,8},{8,9},{9,10},{10,1... | collective-permute-start | bytes 49160 | tf_op jit(solution)/shard_map/ppermute | solution.py:86
  38.3 5.9 %collective-permute-start.11 = (bf16[2,32,128]{2,1,0:T(8,128)(2,1)S(1)}, bf16[2,32,128]{2,1,0:T(8,128)(2,1)S(1)}, u32[]{:S(2)}, u32[]{:S(2)}) collective-permute-start(bf16[2,32,128]{2,1,0:T(8,128)(2,1)S(1)} %collective-permute-done.10), channel_id=1, source_target_pairs={{0,15},{1,0},{2,1},{3,2},{4,3},{5,4},{6,5},{7,6},{8,7},{9,8},{10,9... | collective-permute-start | bytes 49160 | tf_op jit(solution)/shard_map/ppermute | solution.py:88
  42.8 6.1 %collective-permute-start.5 = (bf16[2,32,128]{2,1,0:T(8,128)(2,1)S(1)}, bf16[2,32,128]{2,1,0:T(8,128)(2,1)S(1)}, u32[]{:S(2)}, u32[]{:S(2)}) collective-permute-start(bf16[2,32,128]{2,1,0:T(8,128)(2,1)S(1)} %collective-permute-done.4), channel_id=1, source_target_pairs={{0,1},{1,2},{2,3},{3,4},{4,5},{5,6},{6,7},{7,8},{8,9},{9,10},{10,1... | collective-permute-start | bytes 49160 | tf_op jit(solution)/shard_map/ppermute | solution.py:86
  44.3 5.9 %collective-permute-start.12 = (bf16[2,32,128]{2,1,0:T(8,128)(2,1)S(1)}, bf16[2,32,128]{2,1,0:T(8,128)(2,1)S(1)}, u32[]{:S(2)}, u32[]{:S(2)}) collective-permute-start(bf16[2,32,128]{2,1,0:T(8,128)(2,1)S(1)} %collective-permute-done.11), channel_id=1, source_target_pairs={{0,15},{1,0},{2,1},{3,2},{4,3},{5,4},{6,5},{7,6},{8,7},{9,8},{10,9... | collective-permute-start | bytes 49160 | tf_op jit(solution)/shard_map/ppermute | solution.py:88
  48.9 5.9 %collective-permute-start.6 = (bf16[2,32,128]{2,1,0:T(8,128)(2,1)S(1)}, bf16[2,32,128]{2,1,0:T(8,128)(2,1)S(1)}, u32[]{:S(2)}, u32[]{:S(2)}) collective-permute-start(bf16[2,32,128]{2,1,0:T(8,128)(2,1)S(1)} %collective-permute-done.5), channel_id=1, source_target_pairs={{0,1},{1,2},{2,3},{3,4},{4,5},{5,6},{6,7},{7,8},{8,9},{9,10},{10,1... | collective-permute-start | bytes 49160 | tf_op jit(solution)/shard_map/ppermute | solution.py:86
  50.1 5.9 %collective-permute-start.13 = (bf16[2,32,128]{2,1,0:T(8,128)(2,1)S(1)}, bf16[2,32,128]{2,1,0:T(8,128)(2,1)S(1)}, u32[]{:S(2)}, u32[]{:S(2)}) collective-permute-start(bf16[2,32,128]{2,1,0:T(8,128)(2,1)S(1)} %collective-permute-done.12), channel_id=1, source_target_pairs={{0,15},{1,0},{2,1},{3,2},{4,3},{5,4},{6,5},{7,6},{8,7},{9,8},{10,9... | collective-permute-start | bytes 49160 | tf_op jit(solution)/shard_map/ppermute | solution.py:88
  54.8 5.9 %collective-permute-start.7 = (bf16[2,32,128]{2,1,0:T(8,128)(2,1)S(1)}, bf16[2,32,128]{2,1,0:T(8,128)(2,1)S(1)}, u32[]{:S(2)}, u32[]{:S(2)}) collective-permute-start(bf16[2,32,128]{2,1,0:T(8,128)(2,1)S(1)} %collective-permute-done.6), channel_id=1, source_target_pairs={{0,1},{1,2},{2,3},{3,4},{4,5},{5,6},{6,7},{7,8},{8,9},{9,10},{10,1... | collective-permute-start | bytes 49160 | tf_op jit(solution)/shard_map/ppermute | solution.py:86
  56.0 5.9 %collective-permute-start.14 = (bf16[2,32,128]{2,1,0:T(8,128)(2,1)S(1)}, bf16[2,32,128]{2,1,0:T(8,128)(2,1)S(1)}, u32[]{:S(2)}, u32[]{:S(2)}) collective-permute-start(bf16[2,32,128]{2,1,0:T(8,128)(2,1)S(1)} %collective-permute-done.13), channel_id=1, source_target_pairs={{0,15},{1,0},{2,1},{3,2},{4,3},{5,4},{6,5},{7,6},{8,7},{9,8},{10,9... | collective-permute-start | bytes 49160 | tf_op jit(solution)/shard_map/ppermute | solution.py:88
  62.8 7.6 %copy-start = (s32[2048,128]{1,0:T(8,128)S(1)}, s32[2048,128]{1,0:T(8,128)}, u32[]{:S(2)}) copy-start(s32[2048,128]{1,0:T(8,128)} %param.15) | copy-start | bytes 3145732
  74.4 12.9 %all-to-all-start = ((f32[16,1,1024]{2,1,0:T(1,128)}), f32[16,1,1024]{2,1,0:T(1,128)S(1)}, u32[]{:S(2)}, u32[]{:S(2)}) async-start(f32[16,1,1024]{2,1,0:T(1,128)} %reshape.153), calls=%async_computation | async-start | bytes 131072 | tf_op jit(solution)/shard_map/all_to_all | solution.py:101
Sparse Core Ops, SparseCore 0:
  12.2 42.3 all-gather.1
